TPU v7x, 256 devices: a whole 4x4x8 slice. The times are simulated.
256 devices in a mesh: seq: 32 (over y_lo, z, core), tp: 8 (over x, y_hi).
Axes of the slice: x: 4, y: 4 (y_hi: 2, y_lo: 2; y = y_hi * 2 + y_lo), z: 8, core: 2. Of those that a mesh axis runs over, the one named last changes fastest.
Arguments:
- hidden_in: bfloat16 [4, 2048, 4096], P(None, 'seq'), may hold values from -6 to 6
- ln_gain: float32 [4096], replicated, may hold values from 0.1 to 1.9
- ln_bias: float32 [4096], replicated, may hold values from -3 to 3
- w_qkv: bfloat16 [3, 4096, 4096], P(None, 'seq', 'tp'), may hold values from -0.09375 to 0.09375
- w_out: bfloat16 [4096, 4096], P('tp', 'seq'), may hold values from -1.5 to 1.5
- cache_kv: bfloat16 [4, 512, 2, 4096], P(None, 'seq', None, 'tp'), may hold values from -500 to 500
- cache_len: int32 [4], replicated, may hold values from 128 to 512, as said below
- owner: int32 [8192, 1], P('seq'), may hold values from 0 to 31; in each aligned block of 256 rows (0 to 255, 256 to 511, ...) at most 8 rows name the same one
Outputs:
- attn_out: bfloat16 [4, 2048, 4096], P(None, 'seq', 'tp')
- appended: bfloat16 [8192, 2, 4096], P('seq', None, 'tp')
Inputs may be any that keep to these rules, and one draw needn't show every extreme that they name: `cache_len`: at least 128; one request's cache holds exactly 512 positions. Among the 256 tokens of one device no owner is named more than 8 times.
All inputs are finite; a program needn't handle non-finite values.
Results may differ from a plain program's by a relative error of at most 0.013.
The roundings to bfloat16 on the way count: a program that leaves them out, or rounds other values in their place, can miss the bound.
Values may be sent and summed in bfloat16 or wider, within the bound.
A program may use at most 128 MiB of HBM per device.

v0:
```python
import math

import jax
import jax.numpy as jnp
from jax import lax
from jax.sharding import PartitionSpec as P

HD = 256
ROT = 64
REQ = 4
SLOTS = 8


EPSILON = 1e-05
BASE_FREQ = 10000.0
MASKED = -1e30


def layer_norm(values_in, gain, shift):
    wide = values_in.astype(jnp.float32)
    center = jnp.mean(wide, axis=-1, keepdims=True)
    spread = wide - center
    variance = jnp.mean(spread * spread, axis=-1, keepdims=True)
    return (spread * lax.rsqrt(variance + EPSILON) * gain + shift).astype(jnp.bfloat16)


def rotate(heads_in, positions):
    pair_index = jnp.arange(ROT // 2).astype(jnp.float32)
    inverse = jnp.power(BASE_FREQ, -2.0 * pair_index / ROT)
    angles = positions.astype(jnp.float32)[:, None] * inverse[None, :]
    cosine = jnp.cos(angles)[:, None, :]
    sine = jnp.sin(angles)[:, None, :]
    leading = heads_in.shape[:-1]
    paired = heads_in[..., :ROT].reshape(leading + (ROT // 2, 2))
    even = paired[..., 0]
    odd = paired[..., 1]
    turned = jnp.stack([even * cosine - odd * sine, odd * cosine + even * sine], axis=-1).reshape(
        leading + (ROT,)
    )
    return jnp.concatenate([turned, heads_in[..., ROT:]], axis=-1)


def body(hidden_in, ln_gain, ln_bias, w_qkv, w_out, cache_kv, cache_len, owner):
    new_dev = hidden_in.shape[1]
    tok_rows = REQ * new_dev
    normed = layer_norm(hidden_in.reshape(tok_rows, hidden_in.shape[2]), ln_gain, ln_bias)
    width = w_qkv.shape[2]
    heads_here = width // HD
    seq_count = lax.axis_size("seq")
    seq_here = lax.axis_index("seq")
    cache_each = cache_kv.shape[1]
    cache_dev = REQ * cache_each
    cache_flat = cache_kv.reshape(cache_dev, 2, width)
    rows_dev = cache_dev + tok_rows
    request_ids = jnp.arange(REQ)
    projected = jnp.einsum(
        "tc,icw->itw",
        normed,
        lax.all_gather(w_qkv, "seq", axis=1, tiled=True),
        preferred_element_type=jnp.float32,
    )

    def length_of(requests):
        return jnp.sum(
            jnp.where(requests[:, None] == request_ids[None, :], cache_len[None, :], 0), axis=1
        )

    local_ids = jnp.arange(tok_rows)
    query_req = local_ids // new_dev
    query_pos = length_of(query_req) + seq_here * new_dev + local_ids % new_dev
    shape_heads = (tok_rows, heads_here, HD)
    query = rotate(projected[0].reshape(shape_heads), query_pos).astype(jnp.bfloat16)
    keys_new = (
        rotate(projected[1].reshape(shape_heads), query_pos)
        .astype(jnp.bfloat16)
        .reshape(tok_rows, width)
    )
    values_new = projected[2].astype(jnp.bfloat16)
    fresh = jnp.stack([keys_new, values_new], axis=1)
    local_rows = jnp.concatenate([cache_flat, fresh], axis=0)
    scale_factor = 1.0 / math.sqrt(HD)
    block_rows = lax.all_gather(local_rows, "seq", axis=0, tiled=True)
    highest = jnp.full((heads_here, tok_rows), MASKED, jnp.float32)
    count = block_rows.shape[0]
    row_ids = jnp.arange(count)
    source = jnp.floor_divide(row_ids, rows_dev)
    within = row_ids - source * rows_dev
    in_cache = within < cache_dev
    cache_req = jnp.floor_divide(within, cache_each)
    cache_slot = source * cache_each + within - cache_req * cache_each
    new_local = within - cache_dev
    new_req = jnp.floor_divide(new_local, new_dev)
    key_req = jnp.where(in_cache, cache_req, new_req)
    key_len = length_of(key_req)
    key_pos = jnp.where(
        in_cache, cache_slot, key_len + source * new_dev + new_local - new_req * new_dev
    )
    usable = jnp.logical_or(jnp.logical_not(in_cache), cache_slot < key_len)
    allowed = (
        usable[None, :]
        & (key_req[None, :] == query_req[:, None])
        & (key_pos[None, :] <= query_pos[:, None])
    )
    key_rows = block_rows[:, 0].reshape(count, heads_here, HD)
    value_rows = block_rows[:, 1].reshape(count, heads_here, HD)
    scores = (
        jnp.einsum("qhd,khd->hqk", query, key_rows, preferred_element_type=jnp.float32)
        * scale_factor
    )
    scores = jnp.where(allowed[None], scores, MASKED)
    raised = jnp.maximum(highest, jnp.max(scores, axis=-1))
    weights = jnp.where(allowed[None], jnp.exp(scores - raised[:, :, None]), 0.0)
    weight_sum = jnp.sum(weights, axis=-1)
    weighted = jnp.einsum(
        "hqk,khd->qhd", weights.astype(jnp.bfloat16), value_rows, preferred_element_type=jnp.float32
    )
    highest, weight_sum, weighted = (raised, weight_sum, weighted)
    attended = (
        (weighted / jnp.transpose(weight_sum)[:, :, None])
        .astype(jnp.bfloat16)
        .reshape(tok_rows, width)
    )
    partial_out = jnp.dot(
        attended,
        lax.all_gather(w_out, "seq", axis=1, tiled=True),
        preferred_element_type=jnp.float32,
    ).astype(jnp.bfloat16)
    summed = (
        lax.psum_scatter(partial_out, "tp", scatter_dimension=1, tiled=True)
        .astype(jnp.float32)
        .astype(jnp.bfloat16)
    )
    attn_out = summed.reshape(REQ, new_dev, summed.shape[1])
    owners = owner[:, 0]
    targets = jnp.arange(seq_count)
    marks = (owners[:, None] == targets[None, :]).astype(jnp.int32)
    earlier = jnp.cumsum(marks, axis=0) - marks
    slot_ids = owners * SLOTS + jnp.sum(earlier * marks, axis=1)
    placing = (jnp.arange(seq_count * SLOTS)[:, None] == slot_ids[None, :]).astype(jnp.bfloat16)
    outgoing = jnp.einsum("st,tkw->skw", placing, fresh, preferred_element_type=jnp.float32).astype(
        jnp.bfloat16
    )
    outgoing = outgoing.reshape(seq_count, SLOTS, 2, width)
    arrived = lax.all_to_all(outgoing, "seq", split_axis=0, concat_axis=0, tiled=True)
    appended = arrived.reshape(seq_count * SLOTS, 2, width)
    return (attn_out, appended)


def solution(mesh):
    return jax.shard_map(
        body,
        mesh=mesh,
        in_specs=(
            P(None, "seq", None),
            P(),
            P(),
            P(None, "seq", "tp"),
            P("tp", "seq"),
            P(None, "seq", None, "tp"),
            P(),
            P("seq", None),
        ),
        out_specs=(P(None, "seq", "tp"), P("seq", None, "tp")),
        check_vma=False,
    )
```

profile of v0, /device:TPU:53, one launch (start us, length us, event | category | flops | bytes accessed | tf_op | source)
XLA Modules:
  0.0 397.7 jit_solution(906175402461783005)
XLA Ops:
  7.2 0.0 all-gather.4.cloned.1.call-start
  7.2 0.7 all-gather.4.cloned.1.call-update
  7.9 0.0 all-gather.6.cloned.1.call-start
  7.9 2.0 convert_reduce_fusion
  9.9 0.1 div.119
  10.0 2.3 multiply_reduce_fusion
  12.3 0.1 rsqrt.12
  12.4 0.9 copy.52
  13.3 0.7 select_reduce_fusion.1
  14.1 0.2 multiply_cosine_fusion
  14.3 2.6 fusion.11
  16.9 75.6 %all-gather.4.cloned.1.call-done = bf16[3,4096,512]{2,1,0:T(8,128)(2,1)} async-done(((bf16[3,128,512]{2,1,0:T(8,128)(2,1)}), bf16[3,4096,512]{2,1,0:T(8,128)(2,1)}) %all-gather.4.cloned.1.call-update) | async-done | bytes 12582928 | tf_op jit(solution)/shard_map/all_gather | solution.py:59
  92.5 6.4 %fusion.14 = f32[3,256,512]{2,1,0:T(8,128)S(1)} fusion(bf16[3,4096,512]{2,1,0:T(8,128)(2,1)} %all-gather.4.cloned.1.call-done, bf16[256,4096]{1,0:T(8,128)(2,1)S(1)} %fusion.11), kind=kOutput, calls=%fused_computation.20 | convolution fusion | flops 3221225472 | bytes 16252928 | tf_op jit(solution)/shard_map/tc,icw->itw/dot_general | solution.py:56
  98.9 0.0 copy-start.3
  99.0 0.1 fusion.62
  99.1 0.3 reshape_squeeze.12
  99.4 0.4 slice.90
  99.8 0.1 slice.64
  99.9 0.3 reshape_squeeze.14
  100.2 0.1 slice.71
  100.3 0.1 copy.66
  100.5 0.1 copy.65
  100.6 0.1 subtract_convert_fusion
  100.8 0.2 pad_maximum_fusion.1
  100.9 0.1 copy.54
  101.1 0.6 pad_maximum_fusion
  101.7 0.2 convert_element_type.80
  101.8 0.0 copy-start
  101.9 1.0 maximum_maximum_fusion
  102.8 0.0 all-gather.6.cloned.1.call-update
  102.9 0.0 all-gather.8.cloned.1.call-start
  102.9 0.7 all-gather.8.cloned.1.call-update
  103.6 0.0 reduce-scatter.2.cloned.1.call-start
  103.6 0.1 fusion.50
  103.7 0.0 copy-done.3
  103.7 0.2 select_reduce_fusion
  103.9 0.1 subtract_select_fusion
  104.0 0.1 compare_or_fusion
  104.0 0.0 copy-done
  104.1 2.9 compare_and_fusion
  106.9 0.4 slice.74
  107.3 0.1 copy.57
  107.5 116.5 %all-gather.6.cloned.1.call-done = bf16[10240,2,512]{2,0,1:T(8,128)(2,1)} async-done(((bf16[320,2,512]{2,0,1:T(8,128)(2,1)}), bf16[10240,2,512]{2,0,1:T(8,128)(2,1)}) %all-gather.6.cloned.1.call-update) | async-done | bytes 20971536 | tf_op jit(solution)/shard_map/all_gather | solution.py:82
  224.0 15.6 %fusion.61 = (bf16[10240,1,512]{2,0,1:T(8,128)(2,1)}, bf16[10240,1,512]{2,0,1:T(8,128)(2,1)}) fusion(bf16[10240,2,512]{2,0,1:T(8,128)(2,1)} %all-gather.6.cloned.1.call-done), kind=kLoop, calls=%fused_computation.110 | loop fusion | bytes 41943040 | tf_op jit(solution)/shard_map/slice | solution.py:104
  239.6 13.8 %copy.64 = bf16[10240,1,512]{0,2,1:T(8,128)(2,1)} copy(bf16[10240,1,512]{2,0,1:T(8,128)(2,1)} %get-tuple-element.9) | data formatting | bytes 20971520 | tf_op jit(solution)/shard_map/reshape;squeeze | solution.py:105
  253.4 15.3 %reshape_squeeze.15 = bf16[10240,2,256]{2,1,0:T(2,128)(2,1)} reshape(bf16[10240,1,512]{2,0,1:T(8,128)(2,1)} %get-tuple-element.8) | data formatting | bytes 20971520 | tf_op jit(solution)/shard_map/reshape;squeeze | solution.py:104
  268.7 13.8 %fusion = (f32[2,256]{1,0:T(2,128)S(1)}, f32[2,256,10240]{2,1,0:T(8,128)}) fusion(pred[256,10240]{1,0:T(8,128)(4,1)S(1)} %compare_and_fusion, bf16[10240,2,256]{2,1,0:T(2,128)(2,1)} %reshape_squeeze.15, bf16[256,2,192]{2,0,1:T(8,128)(2,1)S(1)} %copy.74, bf16[256,2,64]{2,0,1:T(8,128)(2,1)S(1)} %copy.57), kind=kOutput, calls=%fused_computation.2 | convolution fusion | flops 2700606976 | bytes 34342912 | tf_op jit(solution)/shard_map/qhd,khd->hqk/dot_general | solution.py:107
  282.5 10.8 %fusion.1 = f32[2,256]{1,0:T(2,128)S(1)} fusion(f32[2,256,10240]{2,1,0:T(8,128)} %get-tuple-element.21, f32[2,256]{1,0:T(2,128)S(1)} %broadcast_maximum_fusion, pred[256,10240]{1,0:T(8,128)(4,1)S(1)} %compare_and_fusion), kind=kLoop, calls=%fused_computation.3 | loop fusion | flops 26213888 | bytes 23597056 | tf_op jit(solution)/shard_map/reduce_sum | solution.py:113
  293.3 0.0 copy-start.2
  293.3 0.0 copy-start.1
  293.3 14.1 %fusion.24 = bf16[256,2,256]{0,2,1:T(8,128)(2,1)S(1)} fusion(bf16[10240,2,256]{0,2,1:T(8,128)(2,1)} %bitcast.69, f32[2,256,10240]{2,1,0:T(8,128)} %get-tuple-element.21, f32[2,256]{1,0:T(2,128)S(1)} %broadcast_maximum_fusion, pred[256,10240]{1,0:T(8,128)(4,1)S(1)} %compare_and_fusion, f32[256,2]{0,1:T(2,128)S(1)} %bitcast.80), kind=kOutput, calls=%fused_computation.25 | convolution fusion | flops 2710831104 | bytes 34344960 | tf_op jit(solution)/shard_map/hqk,khd->qhd/dot_general | solution.py:114
  307.4 0.0 all-gather.8.cloned.1.call-done
  307.5 4.8 %convolution_convert_fusion = bf16[256,4096]{1,0:T(8,128)(2,1)} fusion(bf16[256,512]{0,1:T(8,128)(2,1)S(1)} %bitcast.74, bf16[512,4096]{1,0:T(8,128)(2,1)} %all-gather.8.cloned.1.call-done), kind=kOutput, calls=%fused_computation.10 | convolution fusion | flops 1074790400 | bytes 6553600 | tf_op jit(solution)/shard_map/dot_general | solution.py:123
  312.3 0.0 reduce-scatter.2.cloned.1.call-update
  312.3 0.0 copy-done.2
  312.3 0.6 reduce-window.6
  312.9 0.2 slice_reduce_fusion
  313.1 0.1 fusion.48
  313.2 0.0 copy-done.1
  313.2 0.3 fusion.17
  313.6 0.1 copy.61
  313.6 23.5 %all_to_all.5 = bf16[32,8,2,512]{3,1,2,0:T(8,128)(2,1)S(1)} all-to-all(bf16[32,8,2,512]{3,1,2,0:T(8,128)(2,1)S(1)} %copy.61), channel_id=1, replica_groups=mesh['seq'=32,'tp'=8] {'seq'}, dimensions={0} | all-to-all | bytes 1048576 | tf_op jit(solution)/shard_map/all_to_all | solution.py:144
  337.2 1.3 copy.63
  338.5 52.6 %reduce-scatter.2.cloned.1.call-done = bf16[256,512]{1,0:T(8,128)(2,1)} async-done(((bf16[256,4096]{1,0:T(8,128)(2,1)}), bf16[256,512]{1,0:T(8,128)(2,1)}) %reduce-scatter.2.cloned.1.call-update) | async-done | bytes 262160 | tf_op jit(solution)/shard_map/reduce_scatter | solution.py:129
  (13 shorter events, 0.2 us)
Async XLA Ops:
  7.2 85.4 %all-gather.4.cloned.1.call-start = ((), (), s32[]{:S(2)}) async-start(), calls=%async_computation.2 | async-start | bytes 12976128 | tf_op jit(solution)/shard_map/all_gather | solution.py:59
  7.9 216.1 %all-gather.6.cloned.1.call-start = ((), (), s32[]{:S(2)}) async-start(), calls=%async_computation.3 | async-start | bytes 21626880 | tf_op jit(solution)/shard_map/all_gather | solution.py:82
  98.9 4.8 %copy-start.3 = (s32[4]{0:T(128)S(1)}, s32[4]{0:T(128)}, u32[]{:S(2)}) copy-start(s32[4]{0:T(128)} %param.14) | copy-start | bytes 52
  101.8 2.2 copy-start
  102.9 204.6 %all-gather.8.cloned.1.call-start = ((), (), s32[]{:S(2)}) async-start(), calls=%async_computation.4 | async-start | bytes 4325376 | tf_op jit(solution)/shard_map/all_gather | solution.py:125
  103.6 287.5 %reduce-scatter.2.cloned.1.call-start = ((), (), s32[]{:S(2)}) async-start(), calls=%async_computation.5 | async-start | bytes 2359296 | tf_op jit(solution)/shard_map/reduce_scatter | solution.py:129
  293.3 19.0 %copy-start.2 = (s32[256,1]{0,1:T(1,128)S(1)}, s32[256,1]{0,1:T(1,128)}, u32[]{:S(2)}) copy-start(s32[256,1]{0,1:T(1,128)} %param.15) | copy-start | bytes 3076
  293.3 19.9 %copy-start.1 = (bf16[256,1,512]{2,0,1:T(8,128)(2,1)S(1)}, bf16[256,1,512]{2,0,1:T(8,128)(2,1)}, u32[]{:S(2)}) copy-start(bf16[256,1,512]{2,0,1:T(8,128)(2,1)} %copy-done) | copy-start | bytes 786436
Sparse Core Ops, SparseCore 0:
  9.8 82.6 all-gather.3
  103.0 120.9 all-gather.5
  225.7 72.5 all-gather.7
  312.4 78.6 reduce-scatter.1
where the time goes:
time: 404 us; the launch traced here: 398 us
  waiting for transfers between devices  246 us (61%)
  local copies, waits for them, and re-layouts  49.9 us (12%)
  matrix products  39.4 us (10%)
  other arithmetic  24.5 us (6%)
  blocking collectives  23.5 us (6%)
  between operations  14.1 us (3%)
    all_gather x1, waiting for transfers between devices, body(): block_rows = lax.all_gather(local_rows, 'seq', axis=0, tiled=True)  117 us
    all_gather x1, waiting for transfers between devices, body(): lax.all_gather(w_qkv, 'seq', axis=1, tiled=True)  75.6 us
    reduce_scatter x1, waiting for transfers between devices, body(): lax.psum_scatter(partial_out, 'tp', scatter_dimension=1, tiled=True)  52.6 us
    all_to_all x1, blocking collectives, body(): lax.all_to_all(outgoing, 'seq', split_axis=0, concat_axis=0, tiled=True)  23.5 us
    slice x1, local copies, waits for them, and re-layouts, body(): key_rows = block_rows[:, 0].reshape(count, heads_here, HD)  15.6 us
    another operation x1, local copies, waits for them, and re-layouts, body(): key_rows = block_rows[:, 0].reshape(count, heads_here, HD)  15.3 us
    dot_general x1, matrix products, body(): jnp.einsum('hqk,khd->qhd', weights.astype(jnp.bfloat16), value_rows, pref...  14.1 us
    dot_general x1, matrix products, body(): jnp.einsum('qhd,khd->hqk', query, key_rows, preferred_element_type=jnp.fl...  13.8 us
  transfers between devices with their start and end apart: 4, of which 3 were waited for; matrix products, arithmetic and copies ran while one was open for 25% of the time, Pallas kernels for 0%

commit v1 on v0

v1 whole, which is shorter than its diff:
```python
import jax
import jax.numpy as jnp
import numpy as np
from jax import lax
from jax.experimental import pallas as pl
from jax.experimental.pallas import tpu as pltpu
from jax.sharding import PartitionSpec as P

MESH = pl.DeviceIdType.MESH
HD = 256
ROT = 64
REQ = 4
SLOTS = 8
NZ = 8
EPSILON = 1e-05
BASE_FREQ = 10000.0
MASKED = -1e30
FAR = 1 << 20
BF = jnp.bfloat16
F32 = jnp.float32

R_WY, R_HID, R_CACHE, R_TGT = 0, 1, 3, 4
R_RING = 8
R_SIB = 24
R_Q = 40
R_KV = 44
R_FWD = 48
R_KVS = 52
R_ATT = 60
R_WOR = 68
R_WOY = 76
R_WOS = 88
R_RS = 108
R_APP = 116
N_RECV = 148
N_SEND = 160


def kernel(lens_ref, hid_ref, gain_ref, bias_ref, w_ref, wo_ref, cache_ref, cos_ref, sin_ref, kn_ref, kc_ref,
           orow_ref, ocol_ref, out_ref, app_ref,
           hido, nbuf, wbuf, acc, qs, kvs, qbuf, kvall, attin, ao, wog, pbuf, rbuf, outg, tgt,
           ssem, rsem, lsem):
    s = lax.axis_index("seq")
    t = lax.axis_index("tp")
    y = s // 16
    z = (s // 2) % NZ
    c = s % 2
    oy = 1 - y
    sg = 1 - 2 * (z % 2)
    across = y * 16 * -2 + s + 16
    sib = s + 1 - 2 * c
    t1 = t + 1 - 2 * (t % 2)

    def at_z(zz, yy=None):
        return (y if yy is None else yy) * 16 + zz * 2 + c

    zp = (z + 1) % NZ
    zm = (z + NZ - 1) % NZ
    zpair = z + sg

    barrier = pltpu.get_barrier_semaphore()

    @pl.loop(1, 32)
    def _(k):
        pl.semaphore_signal(barrier, inc=1, device_id={"seq": (s + k) % 32, "tp": t}, device_id_type=MESH)

    @pl.loop(1, 8)
    def _(k):
        pl.semaphore_signal(barrier, inc=1, device_id={"seq": s, "tp": (t + k) % 8}, device_id_type=MESH)

    pl.semaphore_signal(barrier, inc=1, device_id={"seq": across, "tp": t1}, device_id_type=MESH)
    pl.semaphore_wait(barrier, 39)

    sends = []
    locals_ = []

    def put(src, dst, r, seq, tp=None):
        copy = pltpu.make_async_remote_copy(
            src_ref=src, dst_ref=dst, send_sem=ssem.at[len(sends)], recv_sem=rsem.at[r],
            device_id={"seq": seq, "tp": t if tp is None else tp}, device_id_type=MESH)
        copy.start()
        sends.append(copy)

    def got(dst, r):
        pltpu.make_async_copy(dst, dst, rsem.at[r]).wait()

    def here(src, dst):
        copy = pltpu.make_async_copy(src, dst, lsem.at[len(locals_)])
        copy.start()
        locals_.append(copy)
        return copy

    rows_c = pl.ds(pl.multiple_of(c * 128, 128), 128)

    def wblock(yy, zz):
        return wbuf.at[yy, zz, :, rows_c, :]

    own_cols = pl.ds(pl.multiple_of(y * HD, HD), HD)
    oth_cols = pl.ds(pl.multiple_of(oy * HD, HD), HD)
    put(w_ref.at[:, :, oth_cols], wblock(y, z), R_WY, across)
    w_here = here(w_ref.at[:, :, own_cols], wblock(y, z))
    hid_here = here(hid_ref, hido.at[y])
    split = 112
    put(hid_ref.at[pl.ds(0, split)], hido.at[y, pl.ds(0, split)], R_HID, across)
    put(hid_ref.at[pl.ds(split, 256 - split)], hido.at[y, pl.ds(split, 256 - split)], R_HID + 1, across, t1)
    put(cache_ref.at[oy], kvs.at[:, y, pl.ds(64, 16), :], R_CACHE, across)
    cache_here = here(cache_ref.at[y], kvs.at[:, y, pl.ds(64, 16), :])
    wo_cols = pl.ds(pl.multiple_of(c * 128, 128), 128)
    wo_here = here(wo_ref, wog.at[y * NZ + z, :, wo_cols])

    def spread_block(yy, zz, ring, ring_sem, sib_sem):
        block = wblock(yy, zz)
        for target, r in zip(ring, ring_sem):
            put(block, block, r, at_z(target))
        put(block, block, sib_sem, sib)

    w_here.wait()
    spread_block(y, z, (zp, zm), (R_RING, R_RING + 7), R_SIB)

    def layer_norm(yy):
        def step(i, carry):
            rows = pl.ds(pl.multiple_of(i * 16, 16), 16)
            wide = hido[yy, rows, :].astype(F32)
            center = jnp.mean(wide, axis=-1, keepdims=True)
            spread = wide - center
            variance = jnp.mean(spread * spread, axis=-1, keepdims=True)
            nbuf[yy, rows, :] = (spread * lax.rsqrt(variance + EPSILON) * gain_ref[...] + bias_ref[...]).astype(BF)
            return carry
        lax.fori_loop(0, 16, step, 0)

    acc[...] = jnp.zeros_like(acc)

    order = lax.broadcasted_iota(jnp.int32, (256, 256), 0) < lax.broadcasted_iota(jnp.int32, (256, 256), 1)
    same = jnp.where(order & (ocol_ref[...] == orow_ref[...]), 1, 0)
    slot = jnp.sum(same, axis=0, keepdims=True)
    tgt[y] = jnp.broadcast_to(orow_ref[...] * 16 + y * 8 + slot, (8, 256))

    hid_here.wait()
    layer_norm(y)
    put(tgt.at[y], tgt.at[y], R_TGT, across)

    got(wblock(oy, z), R_WY)
    spread_block(oy, z, (zp, zm), (R_RING + 1, R_RING + 8), R_SIB + 1)

    def project(tok_y, yy, zz):
        offset = pl.multiple_of(yy * 2048 + zz * 256, 256)
        left = nbuf[tok_y, :, pl.ds(offset, 256)]

        def step(i, carry):
            acc[i] += jnp.dot(left, wbuf[yy, zz, i], preferred_element_type=F32)
            return carry
        lax.fori_loop(0, 3, step, 0)

    def ring_block(side, k):
        if k < 6:
            d, yy = k // 2 + 1, (y if k % 2 == 0 else oy)
        else:
            d, yy = 4, (y if side == 0 else oy)
        return yy, ((z + NZ - d) % NZ if side == 0 else (z + d) % NZ)

    def sib_wait(yy, zz, r):
        theirs = wbuf.at[yy, zz, :, pl.ds(pl.multiple_of((1 - c) * 128, 128), 128), :]
        got(theirs, r)

    waiting = [(y, z, R_SIB), (oy, z, R_SIB + 1)]
    for k in range(7):
        arrived = []
        for side in (0, 1):
            yy, zz = ring_block(side, k)
            got(wblock(yy, zz), R_RING + side * 7 + k)
            onward = None
            if k < 4:
                onward = k + 2
            elif (k == 4 and side == 0) or (k == 5 and side == 1):
                onward = 6
            ring = () if onward is None else ((zp if side == 0 else zm),)
            ring_sem = () if onward is None else (R_RING + side * 7 + onward,)
            r = R_SIB + 2 + side * 7 + k
            spread_block(yy, zz, ring, ring_sem, r)
            arrived.append((yy, zz, r))
        for yy, zz, r in waiting:
            sib_wait(yy, zz, r)
            project(y, yy, zz)
        waiting = arrived
        if k == 5:
            wo_here.wait()
            mine = wog.at[y * NZ + z, :, wo_cols]
            put(mine, mine, R_WOR, at_z(zp))
            put(mine, mine, R_WOR + 4, at_z(zm))
            put(mine, mine, R_WOY, across)
            put(mine, mine, R_WOS, sib)
            for part in (0, 1):
                rows = pl.ds(0, split) if part == 0 else pl.ds(split, 256 - split)
                got(hido.at[oy, rows], R_HID + part)
            layer_norm(oy)
    for yy, zz, r in waiting:
        sib_wait(yy, zz, r)
        project(y, yy, zz)

    lane = lax.broadcasted_iota(jnp.int32, (64, 128), 1)
    even = lane % 2 == 0

    def finish(tok_y):
        def step(r, carry):
            rows = pl.ds(pl.multiple_of(r * 64, 64), 64)
            cosine = cos_ref[tok_y, rows, :]
            sine = sin_ref[tok_y, rows, :]

            def turn(i):
                head = acc[i, rows, :]
                first = head[:, :128]
                swapped = jnp.where(even, pltpu.roll(first, 127, 1), pltpu.roll(first, 1, 1))
                return jnp.concatenate([first * cosine + swapped * sine, head[:, 128:]], axis=1).astype(BF)

            qs[r, tok_y] = turn(0)
            kvs[r, tok_y, pl.ds(0, 64), pl.ds(0, HD)] = turn(1)
            kvs[r, tok_y, pl.ds(0, 64), pl.ds(HD, HD)] = acc[2, rows, :].astype(BF)
            return carry
        lax.fori_loop(0, REQ, step, 0)

    finish(y)
    acc[...] = jnp.zeros_like(acc)

    def other(n, carry):
        project(oy, n // NZ, n % NZ)
        return carry
    lax.fori_loop(0, 16, other, 0)
    finish(oy)

    got(kvs.at[:, oy, pl.ds(64, 16), :], R_CACHE)
    cache_here.wait()
    q_here = kv_here = None
    for i, off in ((3, -3 * sg), (2, 2 * sg), (1, -sg), (0, 0)):
        dest = (z + off + NZ) % NZ
        r = dest // 2
        if i == 0:
            q_here = here(qs.at[r], qbuf.at[0])
            kv_here = here(kvs.at[r], kvall.at[c, z])
        else:
            put(kvs.at[r], kvall.at[c, z], R_KV + i, at_z(dest))
            put(qs.at[r], qbuf.at[i], R_Q + i, at_z(dest))

    def wo_slot(yy, zz, rows=None):
        return wog.at[yy * NZ + zz, (pl.ds(0, 512) if rows is None else rows), wo_cols]

    def wo_sib_slot(yy, zz, rows=None):
        cols = pl.ds(pl.multiple_of((1 - c) * 128, 128), 128)
        return wog.at[yy * NZ + zz, (pl.ds(0, 512) if rows is None else rows), cols]

    wo_sib = [(wo_sib_slot(y, z), R_WOS)]
    wo_y = [(z, None, R_WOY)]

    def wo_step(d):
        for side in (0, 1):
            zz = (z + NZ - d) % NZ if side == 0 else (z + d) % NZ
            rows = None if d < 4 else pl.ds(side * 256, 256)
            block = wo_slot(y, zz, rows)
            got(block, R_WOR + side * 4 + d - 1)
            if d < 4:
                nxt = block if d < 3 else wo_slot(y, zz, pl.ds(side * 256, 256))
                put(nxt, nxt, R_WOR + side * 4 + d, at_z(zp if side == 0 else zm))
            n = 1 + (d - 1) * 2 + side
            put(block, block, R_WOY + n, across)
            put(block, block, R_WOS + n, sib)
            wo_sib.append((wo_sib_slot(y, zz, rows), R_WOS + n))
            wo_y.append((zz, rows, R_WOY + n))

    wo_step(1)

    got(tgt.at[oy], R_TGT)
    row_id = lax.broadcasted_iota(jnp.int32, (128, 256), 0)

    def place(n, carry):
        total = jnp.zeros((128, 512), F32)
        for yy in (0, 1):
            mark = jnp.where(row_id + n * 128 == tgt[yy, 0:1, :], 1.0, 0.0).astype(BF)
            fresh = kvs[:, yy, 0:64, :].reshape(256, 512)
            total = total + jnp.dot(mark, fresh, preferred_element_type=F32)
        outg[pl.ds(n * 8, 8)] = total.astype(BF).reshape(8, 16, 512)
        return carry
    lax.fori_loop(0, 4, place, 0)
    wo_step(2)

    kv_here.wait()
    for i in range(4):
        src = (z - sg * i + NZ) % NZ
        block = kvall.at[c, src]
        if i > 0:
            got(block, R_KV + i)
        put(block, block, R_FWD + i, at_z(zpair))
        put(block, block, R_KVS + i, sib)
    wo_step(3)
    for i in range(4):
        src = (zpair + sg * i + NZ) % NZ
        block = kvall.at[c, src]
        got(block, R_FWD + i)
        put(block, block, R_KVS + 4 + i, sib)
    wo_step(4)
    for zz, rows, r in wo_y:
        block = wo_slot(oy, zz, rows)
        got(block, r)
        n = r - R_WOY
        put(block, block, R_WOS + 9 + n, sib)
        wo_sib.append((wo_sib_slot(oy, zz, rows), R_WOS + 9 + n))
    for i in range(4):
        got(kvall.at[1 - c, (z - sg * i + NZ) % NZ], R_KVS + i)
        got(kvall.at[1 - c, (zpair + sg * i + NZ) % NZ], R_KVS + 4 + i)
    q_here.wait()
    for i in range(1, 4):
        got(qbuf.at[i], R_Q + i)

    mine_r = z // 2
    length = lens_ref[mine_r]
    row = lax.broadcasted_iota(jnp.int32, (128, 1), 0)

    def attend(i):
        src = (z - sg * i + NZ) % NZ
        query = qbuf[i].reshape(128, HD)
        position = (row // 64) * 1024 + src * 128 + c * 64 + row % 64
        scores = []
        for cc in (0, 1):
            keys = kvall[cc, :, :, :, 0:HD].reshape(1280, HD)
            allowed = (kn_ref[...] + cc * 64 <= position) | (kc_ref[...] + cc * 16 < length)
            score = lax.dot_general(query, keys, (((1,), (1,)), ((), ())), preferred_element_type=F32)
            scores.append(jnp.where(allowed, score * (1.0 / 16.0), MASKED))
        top = jnp.maximum(jnp.max(scores[0], axis=1, keepdims=True), jnp.max(scores[1], axis=1, keepdims=True))
        weight_sum = jnp.zeros((128, 1), F32)
        mixed = jnp.zeros((128, HD), F32)
        for cc in (0, 1):
            weights = jnp.exp(scores[cc] - top)
            weight_sum = weight_sum + jnp.sum(weights, axis=1, keepdims=True)
            values = kvall[cc, :, :, :, HD:2 * HD].reshape(1280, HD)
            mixed = mixed + jnp.dot(weights.astype(BF), values, preferred_element_type=F32)
        ao[i] = (mixed / weight_sum).astype(BF).reshape(2, 64, HD)

    att_here = None
    head_cols = pl.ds(pl.multiple_of(y * HD, HD), HD)
    att_dst = attin.at[mine_r, :, head_cols]
    for i in (3, 2, 1, 0):
        attend(i)
        src = (z - sg * i + NZ) % NZ
        if i > 0:
            put(ao.at[i, y], att_dst, R_ATT + y * 4 + mine_r, at_z(src))
        else:
            att_here = here(ao.at[0, y], att_dst)
        put(ao.at[i, oy], att_dst, R_ATT + y * 4 + mine_r, at_z(src, oy))

    app_here = here(outg.at[s], app_ref.at[s])

    def send_app(k, start):
        dest = (s + k) % 32
        copy = pltpu.make_async_remote_copy(
            src_ref=outg.at[dest], dst_ref=app_ref.at[s], send_sem=ssem.at[N_SEND - 32 + k],
            recv_sem=rsem.at[R_APP + s], device_id={"seq": dest, "tp": t}, device_id_type=MESH)
        if start:
            copy.start()
        else:
            copy.wait_send()

    def app_go(k, carry):
        send_app(k, True)
        return carry
    lax.fori_loop(1, 32, app_go, 0)

    att_here.wait()
    for hh in (0, 1):
        for r in range(REQ):
            slot_ref = attin.at[r, :, pl.ds(hh * HD, HD)]
            mine = (r == mine_r) & (y == hh)

            @pl.when(jnp.logical_not(mine))
            def _():
                got(slot_ref, R_ATT + hh * 4 + r)
    for block, r in wo_sib:
        got(block, r)

    def partial_of(k):
        dest = (t + k) % 8
        left = attin[...].reshape(256, 512)

        def step(h, carry):
            pbuf[k, :, pl.ds(pl.multiple_of(h * 256, 256), 256)] = jnp.dot(
                left, wog[dest * 2 + h], preferred_element_type=F32).astype(BF)
            return carry
        lax.fori_loop(0, 2, step, 0)
        return dest

    for k in range(1, 8):
        dest = partial_of(k)
        put(pbuf.at[k], rbuf.at[k], R_RS + k, s, dest)
    partial_of(0)
    for k in range(1, 8):
        got(rbuf.at[k], R_RS + k)

    def total(i, carry):
        rows = pl.ds(pl.multiple_of(i * 32, 32), 32)
        value = pbuf[0, rows, :].astype(F32)
        for k in range(1, 8):
            value = value + rbuf[k, rows, :].astype(F32)
        out_ref[rows, :] = value.astype(BF)
        return carry
    lax.fori_loop(0, 8, total, 0)

    app_here.wait()

    def app_done(k, carry):
        got(app_ref.at[(s + k) % 32], R_APP + (s + k) % 32)
        send_app(k, False)
        return carry
    lax.fori_loop(1, 32, app_done, 0)
    for copy in sends:
        copy.wait_send()


def body(hidden_in, ln_gain, ln_bias, w_qkv, w_out, cache_kv, cache_len, owner):
    s = lax.axis_index("seq")
    y, zc = s // 16, s % 16
    width = w_qkv.shape[2]
    hid = hidden_in.reshape(256, hidden_in.shape[2])
    cache = jnp.transpose(cache_kv.reshape(REQ, 16, 2, 2, HD), (3, 0, 1, 2, 4)).reshape(2, REQ, 16, 512)

    ids = jnp.arange(64)
    base = (jnp.arange(2) * 16 + zc) * 64
    positions = (cache_len[None, :, None] + base[:, None, None] + ids[None, None, :]).reshape(2, 256)
    pair_index = jnp.arange(ROT // 2).astype(F32)
    inverse = jnp.power(BASE_FREQ, -2.0 * pair_index / ROT)
    angles = positions.astype(F32)[:, :, None] * jnp.repeat(inverse, 2)[None, None, :]
    sign = jnp.where(jnp.arange(ROT) % 2 == 0, -1.0, 1.0)
    cosine = jnp.concatenate([jnp.cos(angles), jnp.ones((2, 256, 64), F32)], axis=-1)
    sine = jnp.concatenate([jnp.sin(angles) * sign, jnp.zeros((2, 256, 64), F32)], axis=-1)

    u = np.arange(1280)
    j, yy, zz = u % 80, (u // 80) % 2, u // 160
    key_new = np.where(j < 64, yy * 1024 + zz * 128 + j, FAR).astype(np.int32)[None]
    key_old = np.where(j < 64, FAR, yy * 256 + zz * 32 + j - 64).astype(np.int32)[None]
    orow = owner.reshape(1, 256)
    vmem = pl.BlockSpec(memory_space=pltpu.VMEM)
    anyw = pl.BlockSpec(memory_space=pl.ANY)
    attn, app = pl.pallas_call(
        kernel,
        out_shape=(jax.ShapeDtypeStruct((256, width), BF), jax.ShapeDtypeStruct((32, 16, 512), BF)),
        in_specs=[pl.BlockSpec(memory_space=pltpu.SMEM), anyw, vmem, vmem, anyw, anyw, anyw,
                  vmem, vmem, vmem, vmem, vmem, vmem],
        out_specs=(vmem, vmem),
        scratch_shapes=[
            pltpu.VMEM((2, 256, 4096), BF),
            pltpu.VMEM((2, 256, 4096), BF),
            pltpu.VMEM((2, NZ, 3, 256, 256), BF),
            pltpu.VMEM((3, 256, 256), F32),
            pltpu.VMEM((REQ, 2, 64, HD), BF),
            pltpu.VMEM((REQ, 2, 80, 512), BF),
            pltpu.VMEM((4, 2, 64, HD), BF),
            pltpu.VMEM((2, NZ, 2, 80, 512), BF),
            pltpu.VMEM((REQ, 64, 512), BF),
            pltpu.VMEM((4, 2, 64, HD), BF),
            pltpu.VMEM((16, 512, 256), BF),
            pltpu.VMEM((8, 256, 512), BF),
            pltpu.VMEM((8, 256, 512), BF),
            pltpu.VMEM((32, 16, 512), BF),
            pltpu.VMEM((2, 8, 256), jnp.int32),
            pltpu.SemaphoreType.DMA((N_SEND,)),
            pltpu.SemaphoreType.DMA((N_RECV,)),
            pltpu.SemaphoreType.DMA((16,)),
        ],
        compiler_params=pltpu.CompilerParams(
            collective_id=0, has_side_effects=True, vmem_limit_bytes=60 * 1024 * 1024),
    )(cache_len, hid, ln_gain.reshape(1, -1), ln_bias.reshape(1, -1), w_qkv, w_out, cache,
      cosine, sine, jnp.asarray(key_new), jnp.asarray(key_old), orow, owner)
    attn_out = attn.reshape(REQ, 64, width)
    app = app.reshape(2, 16, 2, SLOTS, 2, HD)
    appended = jnp.transpose(app, (2, 1, 3, 4, 0, 5)).reshape(256, 2, width)
    return (attn_out, appended)


def solution(mesh):
    return jax.shard_map(
        body,
        mesh=mesh,
        in_specs=(
            P(None, "seq", None),
            P(),
            P(),
            P(None, "seq", "tp"),
            P("tp", "seq"),
            P(None, "seq", None, "tp"),
            P(),
            P("seq", None),
        ),
        out_specs=(P(None, "seq", "tp"), P("seq", None, "tp")),
        check_vma=False,
    )
```

time: 404 us -> 169 us (0.42)
  the two profiles are of different devices: /device:TPU:53 before, /device:TPU:28 now
where the time goes in v1:
time: 169 us; the launch traced here: 168 us
  Pallas kernels  157 us (93%)
  local copies, waits for them, and re-layouts  8.53 us (5%)
  other arithmetic  1.74 us (1%)
    pallas_call x1, Pallas kernels, body(): pl.pallas_call(kernel, out_shape=(jax.ShapeDtypeStruct((256, width), BF),...  157 us

profile of v1, /device:TPU:28, one launch (start us, length us, event | category | flops | bytes accessed | tf_op | source)
XLA Modules:
  0.0 168.3 jit_solution(16753231448658998034)
XLA Ops:
  0.7 0.7 broadcast_add_fusion
  1.4 0.1 add.79
  1.5 0.1 add.76
  1.6 0.1 add.77
  1.6 0.1 broadcast_in_dim.8
  1.7 0.1 mul.42
  1.8 1.0 copy.20
  2.8 0.7 reshape.106.cache_ref
  3.6 1.5 copy.16.ocol_ref
  5.0 1.0 fusion
  6.0 0.7 concatenate.7.sin_ref
  6.8 0.7 concatenate.6.cos_ref
  7.5 157.4 %shard_map.113 = (bf16[256,512]{1,0:T(8,128)(2,1)}, bf16[32,16,512]{2,1,0:T(8,128)(2,1)}) custom-call(s32[4]{0:T(128)} %lens_ref.1, bf16[256,4096]{1,0:T(8,128)(2,1)} %bitcast.15, f32[1,4096]{1,0:T(1,128)} %bitcast.20, f32[1,4096]{1,0:T(1,128)} %bitcast.21, bf16[3,128,512]{2,1,0:T(8,128)(2,1)} %w_ref.1, bf16[512,128]{1,0:T(8,128)(2,1)} %wo_ref.1, ...), custom_call_target="tpu_custom_call" | custom-call | tf_op jit(solution)/shard_map/pallas_call | solution.py:439
  164.9 0.0 copy-start
  164.9 1.6 copy.17
  166.5 1.1 reshape.110
  167.6 0.0 copy-done
  167.6 0.7 copy.22
  (5 shorter events, 0.0 us)
Async XLA Ops:
  164.9 2.8 %copy-start = (bf16[256,512]{1,0:T(8,128)(2,1)S(1)}, bf16[256,512]{1,0:T(8,128)(2,1)}, u32[]{:S(2)}) copy-start(bf16[256,512]{1,0:T(8,128)(2,1)} %get-tuple-element.4) | copy-start | bytes 786436

commit v2 on v1

--- a/solution.py
+++ b/solution.py
@@ -36,9 +36,9 @@
 N_SEND = 160
 
 
-def kernel(lens_ref, hid_ref, gain_ref, bias_ref, w_ref, wo_ref, cache_ref, cos_ref, sin_ref, kn_ref, kc_ref,
-           orow_ref, ocol_ref, out_ref, app_ref,
-           hido, nbuf, wbuf, acc, qs, kvs, qbuf, kvall, attin, ao, wog, pbuf, rbuf, outg, tgt,
+def kernel(lens_ref, hid_ref, gain_ref, bias_ref, w_ref, wo_ref, cache_ref, freq_ref, kn_ref, kc_ref,
+           orow_ref, out_ref, app_ref,
+           hido, nbuf, wbuf, acc, craw, cosb, sinb, qs, kvs, qbuf, kvall, attin, ao, wog, pbuf, rbuf, outg, tgt,
            ssem, rsem, lsem):
     s = lax.axis_index("seq")
     t = lax.axis_index("tp")
@@ -103,8 +103,8 @@
     split = 112
     put(hid_ref.at[pl.ds(0, split)], hido.at[y, pl.ds(0, split)], R_HID, across)
     put(hid_ref.at[pl.ds(split, 256 - split)], hido.at[y, pl.ds(split, 256 - split)], R_HID + 1, across, t1)
-    put(cache_ref.at[oy], kvs.at[:, y, pl.ds(64, 16), :], R_CACHE, across)
-    cache_here = here(cache_ref.at[y], kvs.at[:, y, pl.ds(64, 16), :])
+    put(cache_ref.at[:, :, :, oth_cols], craw.at[y], R_CACHE, across)
+    cache_here = here(cache_ref.at[:, :, :, own_cols], craw.at[y])
     wo_cols = pl.ds(pl.multiple_of(c * 128, 128), 128)
     wo_here = here(wo_ref, wog.at[y * NZ + z, :, wo_cols])
 
@@ -130,24 +130,33 @@
 
     acc[...] = jnp.zeros_like(acc)
 
-    order = lax.broadcasted_iota(jnp.int32, (256, 256), 0) < lax.broadcasted_iota(jnp.int32, (256, 256), 1)
-    same = jnp.where(order & (ocol_ref[...] == orow_ref[...]), 1, 0)
-    slot = jnp.sum(same, axis=0, keepdims=True)
-    tgt[y] = jnp.broadcast_to(orow_ref[...] * 16 + y * 8 + slot, (8, 256))
-
+    def tables():
+        spot = lax.broadcasted_iota(jnp.int32, (64, 128), 0)
+        odd = lax.broadcasted_iota(jnp.int32, (64, 128), 1) % 2
+        for yy in (0, 1):
+            for r in range(REQ):
+                position = spot + (lens_ref[r] + yy * 1024 + z * 128 + c * 64)
+                angle = position.astype(F32) * freq_ref[...]
+                cosb[yy, pl.ds(r * 64, 64), :] = jnp.cos(angle)
+                turned = jnp.sin(angle)
+                sinb[yy, pl.ds(r * 64, 64), :] = jnp.where(odd == 1, turned, -turned)
+        before = lax.broadcasted_iota(jnp.int32, (256, 256), 0) < lax.broadcasted_iota(jnp.int32, (256, 256), 1)
+        across_lanes = jnp.broadcast_to(orow_ref[...].astype(F32), (256, 256))
+        same = jnp.where(before & (jnp.transpose(across_lanes) == across_lanes), 1, 0)
+        slot = jnp.sum(same, axis=0, keepdims=True)
+        tgt[y] = jnp.broadcast_to(orow_ref[...] * 16 + y * 8 + slot, (8, 256))
+
+    got(wblock(oy, z), R_WY)
+    spread_block(oy, z, (zp, zm), (R_RING + 1, R_RING + 8), R_SIB + 1)
     hid_here.wait()
     layer_norm(y)
-    put(tgt.at[y], tgt.at[y], R_TGT, across)
-
-    got(wblock(oy, z), R_WY)
-    spread_block(oy, z, (zp, zm), (R_RING + 1, R_RING + 8), R_SIB + 1)
 
     def project(tok_y, yy, zz):
         offset = pl.multiple_of(yy * 2048 + zz * 256, 256)
         left = nbuf[tok_y, :, pl.ds(offset, 256)]
 
         def step(i, carry):
-            acc[i] += jnp.dot(left, wbuf[yy, zz, i], preferred_element_type=F32)
+            acc[tok_y, i] += jnp.dot(left, wbuf[yy, zz, i], preferred_element_type=F32)
             return carry
         lax.fori_loop(0, 3, step, 0)
 
@@ -182,6 +191,21 @@
             sib_wait(yy, zz, r)
             project(y, yy, zz)
         waiting = arrived
+        if k == 0:
+            tables()
+            put(tgt.at[y], tgt.at[y], R_TGT, across)
+        if k == 2:
+            got(craw.at[oy], R_CACHE)
+            cache_here.wait()
+            for yy in (0, 1):
+                raw = craw[yy]
+                kvs[:, yy, 64:80, 0:HD] = raw[:, :, 0, :]
+                kvs[:, yy, 64:80, HD:2 * HD] = raw[:, :, 1, :]
+        if k == 4:
+            for part in (0, 1):
+                rows = pl.ds(0, split) if part == 0 else pl.ds(split, 256 - split)
+                got(hido.at[oy, rows], R_HID + part)
+            layer_norm(oy)
         if k == 5:
             wo_here.wait()
             mine = wog.at[y * NZ + z, :, wo_cols]
@@ -189,13 +213,19 @@
             put(mine, mine, R_WOR + 4, at_z(zm))
             put(mine, mine, R_WOY, across)
             put(mine, mine, R_WOS, sib)
-            for part in (0, 1):
-                rows = pl.ds(0, split) if part == 0 else pl.ds(split, 256 - split)
-                got(hido.at[oy, rows], R_HID + part)
-            layer_norm(oy)
+
+            def catch_up(n, carry):
+                project(oy, n % 2, (z + NZ - 2 + n // 2) % NZ)
+                return carry
+            lax.fori_loop(0, 10, catch_up, 0)
+            for d in (3, NZ - 3):
+                project(oy, y, (z + d) % NZ)
+    for yy, zz in ((oy, (z + NZ - 3) % NZ), (oy, (z + 3) % NZ)):
+        project(oy, yy, zz)
     for yy, zz, r in waiting:
         sib_wait(yy, zz, r)
         project(y, yy, zz)
+        project(oy, yy, zz)
 
     lane = lax.broadcasted_iota(jnp.int32, (64, 128), 1)
     even = lane % 2 == 0
@@ -203,32 +233,24 @@
     def finish(tok_y):
         def step(r, carry):
             rows = pl.ds(pl.multiple_of(r * 64, 64), 64)
-            cosine = cos_ref[tok_y, rows, :]
-            sine = sin_ref[tok_y, rows, :]
+            cosine = cosb[tok_y, rows, :]
+            sine = sinb[tok_y, rows, :]
 
             def turn(i):
-                head = acc[i, rows, :]
+                head = acc[tok_y, i, rows, :]
                 first = head[:, :128]
                 swapped = jnp.where(even, pltpu.roll(first, 127, 1), pltpu.roll(first, 1, 1))
                 return jnp.concatenate([first * cosine + swapped * sine, head[:, 128:]], axis=1).astype(BF)
 
             qs[r, tok_y] = turn(0)
             kvs[r, tok_y, pl.ds(0, 64), pl.ds(0, HD)] = turn(1)
-            kvs[r, tok_y, pl.ds(0, 64), pl.ds(HD, HD)] = acc[2, rows, :].astype(BF)
+            kvs[r, tok_y, pl.ds(0, 64), pl.ds(HD, HD)] = acc[tok_y, 2, rows, :].astype(BF)
             return carry
         lax.fori_loop(0, REQ, step, 0)
 
     finish(y)
-    acc[...] = jnp.zeros_like(acc)
-
-    def other(n, carry):
-        project(oy, n // NZ, n % NZ)
-        return carry
-    lax.fori_loop(0, 16, other, 0)
     finish(oy)
 
-    got(kvs.at[:, oy, pl.ds(64, 16), :], R_CACHE)
-    cache_here.wait()
     q_here = kv_here = None
     for i, off in ((3, -3 * sg), (2, 2 * sg), (1, -sg), (0, 0)):
         dest = (z + off + NZ) % NZ
@@ -268,18 +290,18 @@
     wo_step(1)
 
     got(tgt.at[oy], R_TGT)
-    row_id = lax.broadcasted_iota(jnp.int32, (128, 256), 0)
+    row_id = lax.broadcasted_iota(jnp.int32, (256, 256), 0)
 
     def place(n, carry):
-        total = jnp.zeros((128, 512), F32)
+        total = jnp.zeros((256, HD), F32)
         for yy in (0, 1):
-            mark = jnp.where(row_id + n * 128 == tgt[yy, 0:1, :], 1.0, 0.0).astype(BF)
-            fresh = kvs[:, yy, 0:64, :].reshape(256, 512)
-            total = total + jnp.dot(mark, fresh, preferred_element_type=F32)
-        outg[pl.ds(n * 8, 8)] = total.astype(BF).reshape(8, 16, 512)
+            for kv in (0, 1):
+                mark = jnp.where(row_id + n * 256 == tgt[yy, 0:1, :] * 2 + kv, 1.0, 0.0).astype(BF)
+                fresh = kvs[:, yy, 0:64, kv * HD:(kv + 1) * HD].reshape(256, HD)
+                total = total + jnp.dot(mark, fresh, preferred_element_type=F32)
+        outg[pl.ds(n * 8, 8)] = total.reshape(8, 2, SLOTS, 2, HD).astype(BF)
         return carry
     lax.fori_loop(0, 4, place, 0)
-    wo_step(2)
 
     kv_here.wait()
     for i in range(4):
@@ -289,19 +311,22 @@
             got(block, R_KV + i)
         put(block, block, R_FWD + i, at_z(zpair))
         put(block, block, R_KVS + i, sib)
-    wo_step(3)
+    wo_step(2)
     for i in range(4):
         src = (zpair + sg * i + NZ) % NZ
         block = kvall.at[c, src]
         got(block, R_FWD + i)
         put(block, block, R_KVS + 4 + i, sib)
-    wo_step(4)
-    for zz, rows, r in wo_y:
-        block = wo_slot(oy, zz, rows)
-        got(block, r)
-        n = r - R_WOY
-        put(block, block, R_WOS + 9 + n, sib)
-        wo_sib.append((wo_sib_slot(oy, zz, rows), R_WOS + 9 + n))
+    wo_step(3)
+
+    def wo_onward(which):
+        for zz, rows, r in which:
+            block = wo_slot(oy, zz, rows)
+            got(block, r)
+            n = r - R_WOY
+            put(block, block, R_WOS + 9 + n, sib)
+            wo_sib.append((wo_sib_slot(oy, zz, rows), R_WOS + 9 + n))
+
     for i in range(4):
         got(kvall.at[1 - c, (z - sg * i + NZ) % NZ], R_KVS + i)
         got(kvall.at[1 - c, (zpair + sg * i + NZ) % NZ], R_KVS + 4 + i)
@@ -344,13 +369,18 @@
         else:
             att_here = here(ao.at[0, y], att_dst)
         put(ao.at[i, oy], att_dst, R_ATT + y * 4 + mine_r, at_z(src, oy))
-
-    app_here = here(outg.at[s], app_ref.at[s])
+        if i == 3:
+            wo_step(4)
+        if i == 2:
+            wo_onward(wo_y[:5])
+
+    head_cols_of = pl.ds(pl.multiple_of(y * HD, HD), HD)
+    app_here = here(outg.at[s], app_ref.at[:, s % 16, :, :, head_cols_of])
 
     def send_app(k, start):
         dest = (s + k) % 32
         copy = pltpu.make_async_remote_copy(
-            src_ref=outg.at[dest], dst_ref=app_ref.at[s], send_sem=ssem.at[N_SEND - 32 + k],
+            src_ref=outg.at[dest], dst_ref=app_ref.at[:, s % 16, :, :, head_cols_of], send_sem=ssem.at[N_SEND - 32 + k],
             recv_sem=rsem.at[R_APP + s], device_id={"seq": dest, "tp": t}, device_id_type=MESH)
         if start:
             copy.start()
@@ -371,6 +401,7 @@
             @pl.when(jnp.logical_not(mine))
             def _():
                 got(slot_ref, R_ATT + hh * 4 + r)
+    wo_onward(wo_y[5:])
     for block, r in wo_sib:
         got(block, r)
 
@@ -404,7 +435,9 @@
     app_here.wait()
 
     def app_done(k, carry):
-        got(app_ref.at[(s + k) % 32], R_APP + (s + k) % 32)
+        o = (s + k) % 32
+        cols = pl.ds(pl.multiple_of(o // 16 * HD, HD), HD)
+        got(app_ref.at[:, o % 16, :, :, cols], R_APP + o)
         send_app(k, False)
         return carry
     lax.fori_loop(1, 32, app_done, 0)
@@ -413,22 +446,10 @@
 
 
 def body(hidden_in, ln_gain, ln_bias, w_qkv, w_out, cache_kv, cache_len, owner):
-    s = lax.axis_index("seq")
-    y, zc = s // 16, s % 16
     width = w_qkv.shape[2]
     hid = hidden_in.reshape(256, hidden_in.shape[2])
-    cache = jnp.transpose(cache_kv.reshape(REQ, 16, 2, 2, HD), (3, 0, 1, 2, 4)).reshape(2, REQ, 16, 512)
-
-    ids = jnp.arange(64)
-    base = (jnp.arange(2) * 16 + zc) * 64
-    positions = (cache_len[None, :, None] + base[:, None, None] + ids[None, None, :]).reshape(2, 256)
-    pair_index = jnp.arange(ROT // 2).astype(F32)
-    inverse = jnp.power(BASE_FREQ, -2.0 * pair_index / ROT)
-    angles = positions.astype(F32)[:, :, None] * jnp.repeat(inverse, 2)[None, None, :]
-    sign = jnp.where(jnp.arange(ROT) % 2 == 0, -1.0, 1.0)
-    cosine = jnp.concatenate([jnp.cos(angles), jnp.ones((2, 256, 64), F32)], axis=-1)
-    sine = jnp.concatenate([jnp.sin(angles) * sign, jnp.zeros((2, 256, 64), F32)], axis=-1)
-
+    pair = np.arange(128) // 2
+    freq = np.where(pair < ROT // 2, BASE_FREQ ** (-2.0 * pair / ROT), 0.0).astype(np.float32)[None]
     u = np.arange(1280)
     j, yy, zz = u % 80, (u // 80) % 2, u // 160
     key_new = np.where(j < 64, yy * 1024 + zz * 128 + j, FAR).astype(np.int32)[None]
@@ -438,15 +459,18 @@
     anyw = pl.BlockSpec(memory_space=pl.ANY)
     attn, app = pl.pallas_call(
         kernel,
-        out_shape=(jax.ShapeDtypeStruct((256, width), BF), jax.ShapeDtypeStruct((32, 16, 512), BF)),
+        out_shape=(jax.ShapeDtypeStruct((256, width), BF), jax.ShapeDtypeStruct((2, 16, SLOTS, 2, width), BF)),
         in_specs=[pl.BlockSpec(memory_space=pltpu.SMEM), anyw, vmem, vmem, anyw, anyw, anyw,
-                  vmem, vmem, vmem, vmem, vmem, vmem],
+                  vmem, vmem, vmem, vmem],
         out_specs=(vmem, vmem),
         scratch_shapes=[
             pltpu.VMEM((2, 256, 4096), BF),
             pltpu.VMEM((2, 256, 4096), BF),
             pltpu.VMEM((2, NZ, 3, 256, 256), BF),
-            pltpu.VMEM((3, 256, 256), F32),
+            pltpu.VMEM((2, 3, 256, 256), F32),
+            pltpu.VMEM((2, REQ, 16, 2, HD), BF),
+            pltpu.VMEM((2, 256, 128), F32),
+            pltpu.VMEM((2, 256, 128), F32),
             pltpu.VMEM((REQ, 2, 64, HD), BF),
             pltpu.VMEM((REQ, 2, 80, 512), BF),
             pltpu.VMEM((4, 2, 64, HD), BF),
@@ -456,7 +480,7 @@
             pltpu.VMEM((16, 512, 256), BF),
             pltpu.VMEM((8, 256, 512), BF),
             pltpu.VMEM((8, 256, 512), BF),
-            pltpu.VMEM((32, 16, 512), BF),
+            pltpu.VMEM((32, 2, SLOTS, 2, HD), BF),
             pltpu.VMEM((2, 8, 256), jnp.int32),
             pltpu.SemaphoreType.DMA((N_SEND,)),
             pltpu.SemaphoreType.DMA((N_RECV,)),
@@ -464,11 +488,10 @@
         ],
         compiler_params=pltpu.CompilerParams(
             collective_id=0, has_side_effects=True, vmem_limit_bytes=60 * 1024 * 1024),
-    )(cache_len, hid, ln_gain.reshape(1, -1), ln_bias.reshape(1, -1), w_qkv, w_out, cache,
-      cosine, sine, jnp.asarray(key_new), jnp.asarray(key_old), orow, owner)
+    )(cache_len, hid, ln_gain.reshape(1, -1), ln_bias.reshape(1, -1), w_qkv, w_out, cache_kv,
+      jnp.asarray(freq), jnp.asarray(key_new), jnp.asarray(key_old), orow)
     attn_out = attn.reshape(REQ, 64, width)
-    app = app.reshape(2, 16, 2, SLOTS, 2, HD)
-    appended = jnp.transpose(app, (2, 1, 3, 4, 0, 5)).reshape(256, 2, width)
+    appended = app.reshape(256, 2, width)
     return (attn_out, appended)
 
 

time: 169 us -> 154 us (0.911)
  the two profiles are of different devices: /device:TPU:28 before, /device:TPU:53 now
where the time goes in v2:
time: 154 us; the launch traced here: 152 us
  Pallas kernels  148 us (96%)
  local copies, waits for them, and re-layouts  3.86 us (3%)
    pallas_call x1, Pallas kernels, body(): pl.pallas_call(kernel, out_shape=(jax.ShapeDtypeStruct((256, width), BF),...  148 us
    unnamed x2, local copies, waits for them, and re-layouts  3.86 us

profile of v2, /device:TPU:53, one launch (start us, length us, event | category | flops | bytes accessed | tf_op | source)
XLA Modules:
  0.0 152.1 jit_solution(9914387069609857365)
XLA Ops:
  0.6 147.6 %shard_map.122 = (bf16[256,512]{1,0:T(8,128)(2,1)}, bf16[2,16,8,2,512]{4,3,2,1,0:T(2,128)(2,1)}) custom-call(s32[4]{0:T(128)} %lens_ref.1, bf16[256,4096]{1,0:T(8,128)(2,1)} %bitcast.6, f32[1,4096]{1,0:T(1,128)} %bitcast.9, f32[1,4096]{1,0:T(1,128)} %bitcast.10, bf16[3,128,512]{2,1,0:T(8,128)(2,1)} %w_ref.1, bf16[512,128]{1,0:T(8,128)(2,1)} %wo_ref.1, ...), custom_call_target="tpu_custom_call" | custom-call | tf_op jit(solution)/shard_map/pallas_call | solution.py:460
  148.3 1.7 %copy.15 = bf16[4,64,512]{2,1,0:T(8,128)(2,1)} copy(bf16[4,64,512]{2,1,0:T(8,128)(2,1)} %bitcast.8) | data formatting | bytes 524288
  149.9 2.2 %copy.16 = bf16[256,2,512]{2,1,0:T(2,128)(2,1)} copy(bf16[256,2,512]{2,1,0:T(2,128)(2,1)} %bitcast.7) | data formatting | bytes 1048576

commit v3 on v2

--- a/solution.py
+++ b/solution.py
@@ -19,21 +19,21 @@
 BF = jnp.bfloat16
 F32 = jnp.float32
 
-R_WY, R_HID, R_CACHE, R_TGT = 0, 1, 3, 4
+R_WY, R_CACHE, R_TGT, R_HID = 0, 1, 2, 4
 R_RING = 8
-R_SIB = 24
-R_Q = 40
-R_KV = 44
-R_FWD = 48
-R_KVS = 52
-R_ATT = 60
-R_WOR = 68
-R_WOY = 76
-R_WOS = 88
-R_RS = 108
-R_APP = 116
-N_RECV = 148
-N_SEND = 160
+R_SIB = 22
+R_Q = 38
+R_KV = 46
+R_FWD = 54
+R_KVS = 62
+R_ATT = 78
+R_WOR = 86
+R_WOY = 94
+R_WOS = 103
+R_RS = 121
+R_APP = 129
+N_RECV = 161
+N_SEND = 192
 
 
 def kernel(lens_ref, hid_ref, gain_ref, bias_ref, w_ref, wo_ref, cache_ref, freq_ref, kn_ref, kc_ref,
@@ -100,9 +100,9 @@
     put(w_ref.at[:, :, oth_cols], wblock(y, z), R_WY, across)
     w_here = here(w_ref.at[:, :, own_cols], wblock(y, z))
     hid_here = here(hid_ref, hido.at[y])
-    split = 112
-    put(hid_ref.at[pl.ds(0, split)], hido.at[y, pl.ds(0, split)], R_HID, across)
-    put(hid_ref.at[pl.ds(split, 256 - split)], hido.at[y, pl.ds(split, 256 - split)], R_HID + 1, across, t1)
+    hid_rows = ((0, 64, t), (64, 64, t1), (128, 48, t), (176, 80, t1))
+    for n, (first, count, via) in enumerate(hid_rows):
+        put(hid_ref.at[pl.ds(first, count)], hido.at[y, pl.ds(first, count)], R_HID + n, across, via)
     put(cache_ref.at[:, :, :, oth_cols], craw.at[y], R_CACHE, across)
     cache_here = here(cache_ref.at[:, :, :, own_cols], craw.at[y])
     wo_cols = pl.ds(pl.multiple_of(c * 128, 128), 128)
@@ -117,7 +117,7 @@
     w_here.wait()
     spread_block(y, z, (zp, zm), (R_RING, R_RING + 7), R_SIB)
 
-    def layer_norm(yy):
+    def layer_norm(yy, first=0, count=256):
         def step(i, carry):
             rows = pl.ds(pl.multiple_of(i * 16, 16), 16)
             wide = hido[yy, rows, :].astype(F32)
@@ -126,7 +126,7 @@
             variance = jnp.mean(spread * spread, axis=-1, keepdims=True)
             nbuf[yy, rows, :] = (spread * lax.rsqrt(variance + EPSILON) * gain_ref[...] + bias_ref[...]).astype(BF)
             return carry
-        lax.fori_loop(0, 16, step, 0)
+        lax.fori_loop(first // 16, (first + count) // 16, step, 0)
 
     acc[...] = jnp.zeros_like(acc)
 
@@ -151,14 +151,13 @@
     hid_here.wait()
     layer_norm(y)
 
-    def project(tok_y, yy, zz):
+    def project(tok_y, yy, zz, first=0, count=256):
         offset = pl.multiple_of(yy * 2048 + zz * 256, 256)
-        left = nbuf[tok_y, :, pl.ds(offset, 256)]
-
-        def step(i, carry):
-            acc[tok_y, i] += jnp.dot(left, wbuf[yy, zz, i], preferred_element_type=F32)
-            return carry
-        lax.fori_loop(0, 3, step, 0)
+        rows = pl.ds(first, count)
+        left = nbuf[tok_y, rows, pl.ds(offset, 256)]
+
+        for i in range(3):
+            acc[tok_y, i, rows, :] += jnp.dot(left, wbuf[yy, zz, i], preferred_element_type=F32)
 
     def ring_block(side, k):
         if k < 6:
@@ -201,31 +200,32 @@
                 raw = craw[yy]
                 kvs[:, yy, 64:80, 0:HD] = raw[:, :, 0, :]
                 kvs[:, yy, 64:80, HD:2 * HD] = raw[:, :, 1, :]
-        if k == 4:
-            for part in (0, 1):
-                rows = pl.ds(0, split) if part == 0 else pl.ds(split, 256 - split)
-                got(hido.at[oy, rows], R_HID + part)
-            layer_norm(oy)
-        if k == 5:
-            wo_here.wait()
-            mine = wog.at[y * NZ + z, :, wo_cols]
-            put(mine, mine, R_WOR, at_z(zp))
-            put(mine, mine, R_WOR + 4, at_z(zm))
-            put(mine, mine, R_WOY, across)
-            put(mine, mine, R_WOS, sib)
+        if k == 3 or k == 5:
+            n = k - 3
+            if k == 5:
+                wo_here.wait()
+                mine = wog.at[y * NZ + z, :, wo_cols]
+                put(mine, mine, R_WOR, at_z(zp))
+                put(mine, mine, R_WOR + 4, at_z(zm))
+                put(mine, mine, R_WOY, across)
+                put(mine, mine, R_WOS, sib)
+            for part in (n, n + 1):
+                first, count, _ = hid_rows[part]
+                got(hido.at[oy, pl.ds(first, count)], R_HID + part)
+            layer_norm(oy, n * 64, 128)
+        if k == 4 or k == 5:
+            half = (k - 4) * 128
 
             def catch_up(n, carry):
-                project(oy, n % 2, (z + NZ - 2 + n // 2) % NZ)
+                project(oy, n % 2, (z + NZ - 2 + n // 2) % NZ, half, 128)
                 return carry
             lax.fori_loop(0, 10, catch_up, 0)
+        if k == 5:
             for d in (3, NZ - 3):
                 project(oy, y, (z + d) % NZ)
-    for yy, zz in ((oy, (z + NZ - 3) % NZ), (oy, (z + 3) % NZ)):
-        project(oy, yy, zz)
     for yy, zz, r in waiting:
         sib_wait(yy, zz, r)
         project(y, yy, zz)
-        project(oy, yy, zz)
 
     lane = lax.broadcasted_iota(jnp.int32, (64, 128), 1)
     even = lane % 2 == 0
@@ -248,19 +248,40 @@
             return carry
         lax.fori_loop(0, REQ, step, 0)
 
+    def send_round(h, yy):
+        held = []
+        hops = ((3, (z - 3 * sg + NZ) % NZ), (2, (z + 2 * sg + NZ) % NZ), (1, (z - sg + NZ) % NZ))
+        for i, dest in hops:
+            put(kvs.at[dest // 2, yy], kvall.at[c, z, yy], R_KV + h * 4 + i, at_z(dest))
+        for i, dest in hops:
+            put(qs.at[dest // 2, yy], qbuf.at[i, yy], R_Q + h * 4 + i, at_z(dest))
+        held.append(here(kvs.at[z // 2, yy], kvall.at[c, z, yy]))
+        held.append(here(qs.at[z // 2, yy], qbuf.at[0, yy]))
+        return held
+
+    def forward_round(h, yy, held):
+        held[0].wait()
+        for i in range(4):
+            block = kvall.at[c, (z - sg * i + NZ) % NZ, yy]
+            if i > 0:
+                got(block, R_KV + h * 4 + i)
+            put(block, block, R_FWD + h * 4 + i, at_z(zpair))
+            put(block, block, R_KVS + h * 8 + i, sib)
+
+    def sibling_round(h, yy):
+        for i in range(4):
+            block = kvall.at[c, (zpair + sg * i + NZ) % NZ, yy]
+            got(block, R_FWD + h * 4 + i)
+            put(block, block, R_KVS + h * 8 + 4 + i, sib)
+
     finish(y)
+    held_own = send_round(0, y)
+    for yy, zz in ((oy, (z + NZ - 3) % NZ), (oy, (z + 3) % NZ)):
+        project(oy, yy, zz)
+    for yy, zz, r in waiting:
+        project(oy, yy, zz)
     finish(oy)
-
-    q_here = kv_here = None
-    for i, off in ((3, -3 * sg), (2, 2 * sg), (1, -sg), (0, 0)):
-        dest = (z + off + NZ) % NZ
-        r = dest // 2
-        if i == 0:
-            q_here = here(qs.at[r], qbuf.at[0])
-            kv_here = here(kvs.at[r], kvall.at[c, z])
-        else:
-            put(kvs.at[r], kvall.at[c, z], R_KV + i, at_z(dest))
-            put(qs.at[r], qbuf.at[i], R_Q + i, at_z(dest))
+    held_oth = send_round(1, oy)
 
     def wo_slot(yy, zz, rows=None):
         return wog.at[yy * NZ + zz, (pl.ds(0, 512) if rows is None else rows), wo_cols]
@@ -288,6 +309,7 @@
             wo_y.append((zz, rows, R_WOY + n))
 
     wo_step(1)
+    forward_round(0, y, held_own)
 
     got(tgt.at[oy], R_TGT)
     row_id = lax.broadcasted_iota(jnp.int32, (256, 256), 0)
@@ -303,20 +325,10 @@
         return carry
     lax.fori_loop(0, 4, place, 0)
 
-    kv_here.wait()
-    for i in range(4):
-        src = (z - sg * i + NZ) % NZ
-        block = kvall.at[c, src]
-        if i > 0:
-            got(block, R_KV + i)
-        put(block, block, R_FWD + i, at_z(zpair))
-        put(block, block, R_KVS + i, sib)
+    sibling_round(0, y)
+    forward_round(1, oy, held_oth)
     wo_step(2)
-    for i in range(4):
-        src = (zpair + sg * i + NZ) % NZ
-        block = kvall.at[c, src]
-        got(block, R_FWD + i)
-        put(block, block, R_KVS + 4 + i, sib)
+    sibling_round(1, oy)
     wo_step(3)
 
     def wo_onward(which):
@@ -327,12 +339,32 @@
             put(block, block, R_WOS + 9 + n, sib)
             wo_sib.append((wo_sib_slot(oy, zz, rows), R_WOS + 9 + n))
 
-    for i in range(4):
-        got(kvall.at[1 - c, (z - sg * i + NZ) % NZ], R_KVS + i)
-        got(kvall.at[1 - c, (zpair + sg * i + NZ) % NZ], R_KVS + 4 + i)
-    q_here.wait()
-    for i in range(1, 4):
-        got(qbuf.at[i], R_Q + i)
+    for h, yy in ((0, y), (1, oy)):
+        for i in range(4):
+            got(kvall.at[1 - c, (z - sg * i + NZ) % NZ, yy], R_KVS + h * 8 + i)
+            got(kvall.at[1 - c, (zpair + sg * i + NZ) % NZ, yy], R_KVS + h * 8 + 4 + i)
+            if i > 0:
+                got(qbuf.at[i, yy], R_Q + h * 4 + i)
+    held_own[1].wait()
+    held_oth[1].wait()
+
+    head_cols_of = pl.ds(pl.multiple_of(y * HD, HD), HD)
+
+    def send_app(n, start):
+        dest = jnp.where(n < 16, oy, y) * 16 + (s + n) % 16
+        copy = pltpu.make_async_remote_copy(
+            src_ref=outg.at[dest], dst_ref=app_ref.at[:, s % 16, :, :, head_cols_of],
+            send_sem=ssem.at[N_SEND - 32 + n], recv_sem=rsem.at[R_APP + s],
+            device_id={"seq": dest, "tp": t}, device_id_type=MESH)
+        if start:
+            copy.start()
+        else:
+            copy.wait_send()
+
+    def app_go(n, carry):
+        send_app(n, True)
+        return carry
+    lax.fori_loop(0, 16, app_go, 0)
 
     mine_r = z // 2
     length = lens_ref[mine_r]
@@ -374,24 +406,7 @@
         if i == 2:
             wo_onward(wo_y[:5])
 
-    head_cols_of = pl.ds(pl.multiple_of(y * HD, HD), HD)
     app_here = here(outg.at[s], app_ref.at[:, s % 16, :, :, head_cols_of])
-
-    def send_app(k, start):
-        dest = (s + k) % 32
-        copy = pltpu.make_async_remote_copy(
-            src_ref=outg.at[dest], dst_ref=app_ref.at[:, s % 16, :, :, head_cols_of], send_sem=ssem.at[N_SEND - 32 + k],
-            recv_sem=rsem.at[R_APP + s], device_id={"seq": dest, "tp": t}, device_id_type=MESH)
-        if start:
-            copy.start()
-        else:
-            copy.wait_send()
-
-    def app_go(k, carry):
-        send_app(k, True)
-        return carry
-    lax.fori_loop(1, 32, app_go, 0)
-
     att_here.wait()
     for hh in (0, 1):
         for r in range(REQ):
@@ -409,16 +424,14 @@
         dest = (t + k) % 8
         left = attin[...].reshape(256, 512)
 
-        def step(h, carry):
-            pbuf[k, :, pl.ds(pl.multiple_of(h * 256, 256), 256)] = jnp.dot(
-                left, wog[dest * 2 + h], preferred_element_type=F32).astype(BF)
-            return carry
-        lax.fori_loop(0, 2, step, 0)
+        for h in range(2):
+            pbuf[k, :, pl.ds(h * 256, 256)] = jnp.dot(left, wog[dest * 2 + h], preferred_element_type=F32).astype(BF)
         return dest
 
     for k in range(1, 8):
         dest = partial_of(k)
         put(pbuf.at[k], rbuf.at[k], R_RS + k, s, dest)
+    lax.fori_loop(17, 32, app_go, 0)
     partial_of(0)
     for k in range(1, 8):
         got(rbuf.at[k], R_RS + k)
@@ -438,9 +451,14 @@
         o = (s + k) % 32
         cols = pl.ds(pl.multiple_of(o // 16 * HD, HD), HD)
         got(app_ref.at[:, o % 16, :, :, cols], R_APP + o)
-        send_app(k, False)
         return carry
     lax.fori_loop(1, 32, app_done, 0)
+
+    def app_sent(n, carry):
+        send_app(n, False)
+        return carry
+    lax.fori_loop(0, 16, app_sent, 0)
+    lax.fori_loop(17, 32, app_sent, 0)
     for copy in sends:
         copy.wait_send()
 

time: 154 us -> 147 us (0.955); the launches traced: 152 us -> 147 us
  Pallas kernels: 148 us -> 142 us
    pallas_call x1, Pallas kernels: 148 us -> 142 us  [body(): pl.pallas_call(kernel, out_shape=(jax.ShapeDtypeStruct((256, width), BF),...]
where the time goes in v3:
time: 147 us
  Pallas kernels  142 us (97%)
  local copies, waits for them, and re-layouts  3.86 us (3%)
    pallas_call x1, Pallas kernels, body(): pl.pallas_call(kernel, out_shape=(jax.ShapeDtypeStruct((256, width), BF),...  142 us
    unnamed x2, local copies, waits for them, and re-layouts  3.86 us

profile of v3, /device:TPU:53, one launch (start us, length us, event | category | flops | bytes accessed | tf_op | source)
XLA Modules:
  0.0 146.7 jit_solution(9586229990555079576)
XLA Ops:
  0.6 142.2 %shard_map.122 = (bf16[256,512]{1,0:T(8,128)(2,1)}, bf16[2,16,8,2,512]{4,3,2,1,0:T(2,128)(2,1)}) custom-call(s32[4]{0:T(128)} %lens_ref.1, bf16[256,4096]{1,0:T(8,128)(2,1)} %bitcast.6, f32[1,4096]{1,0:T(1,128)} %bitcast.9, f32[1,4096]{1,0:T(1,128)} %bitcast.10, bf16[3,128,512]{2,1,0:T(8,128)(2,1)} %w_ref.1, bf16[512,128]{1,0:T(8,128)(2,1)} %wo_ref.1, ...), custom_call_target="tpu_custom_call" | custom-call | tf_op jit(solution)/shard_map/pallas_call | solution.py:478
  142.9 1.7 %copy.15 = bf16[4,64,512]{2,1,0:T(8,128)(2,1)} copy(bf16[4,64,512]{2,1,0:T(8,128)(2,1)} %bitcast.8) | data formatting | bytes 524288
  144.5 2.2 %copy.16 = bf16[256,2,512]{2,1,0:T(2,128)(2,1)} copy(bf16[256,2,512]{2,1,0:T(2,128)(2,1)} %bitcast.7) | data formatting | bytes 1048576

commit v4 on v3

--- a/solution.py
+++ b/solution.py
@@ -39,7 +39,7 @@
 def kernel(lens_ref, hid_ref, gain_ref, bias_ref, w_ref, wo_ref, cache_ref, freq_ref, kn_ref, kc_ref,
            orow_ref, out_ref, app_ref,
            hido, nbuf, wbuf, acc, craw, cosb, sinb, qs, kvs, qbuf, kvall, attin, ao, wog, pbuf, rbuf, outg, tgt,
-           ssem, rsem, lsem):
+           ssem, rsem, lsem, meet):
     s = lax.axis_index("seq")
     t = lax.axis_index("tp")
     y = s // 16
@@ -59,17 +59,18 @@
     zpair = z + sg
 
     barrier = pltpu.get_barrier_semaphore()
-
-    @pl.loop(1, 32)
-    def _(k):
-        pl.semaphore_signal(barrier, inc=1, device_id={"seq": (s + k) % 32, "tp": t}, device_id_type=MESH)
-
-    @pl.loop(1, 8)
-    def _(k):
-        pl.semaphore_signal(barrier, inc=1, device_id={"seq": s, "tp": (t + k) % 8}, device_id_type=MESH)
-
-    pl.semaphore_signal(barrier, inc=1, device_id={"seq": across, "tp": t1}, device_id_type=MESH)
-    pl.semaphore_wait(barrier, 39)
+    tps = ((t + 2) % 8, (t + 6) % 8)
+    near = [(at_z(zp), t), (at_z(zm), t), (sib, t), (across, t), (across, t1)] + [(s, tt) for tt in tps]
+    for ss, tt in near:
+        pl.semaphore_signal(barrier, inc=1, device_id={"seq": ss, "tp": tt}, device_id_type=MESH)
+    pl.semaphore_wait(barrier, 7)
+
+    def meet_signal(n):
+        for ss, tt in [(s, tt) for tt in tps] + ([(across, t1)] if n == 0 else []):
+            pl.semaphore_signal(meet.at[n], inc=1, device_id={"seq": ss, "tp": tt}, device_id_type=MESH)
+
+    def meet_wait(n):
+        pl.semaphore_wait(meet.at[n], 3 if n == 0 else 2)
 
     sends = []
     locals_ = []
@@ -114,6 +115,7 @@
             put(block, block, r, at_z(target))
         put(block, block, sib_sem, sib)
 
+    meet_signal(0)
     w_here.wait()
     spread_block(y, z, (zp, zm), (R_RING, R_RING + 7), R_SIB)
 
@@ -149,7 +151,7 @@
     got(wblock(oy, z), R_WY)
     spread_block(oy, z, (zp, zm), (R_RING + 1, R_RING + 8), R_SIB + 1)
     hid_here.wait()
-    layer_norm(y)
+    layer_norm(y, 0, 128)
 
     def project(tok_y, yy, zz, first=0, count=256):
         offset = pl.multiple_of(yy * 2048 + zz * 256, 256)
@@ -186,6 +188,8 @@
             r = R_SIB + 2 + side * 7 + k
             spread_block(yy, zz, ring, ring_sem, r)
             arrived.append((yy, zz, r))
+        if k == 0:
+            layer_norm(y, 128, 128)
         for yy, zz, r in waiting:
             sib_wait(yy, zz, r)
             project(y, yy, zz)
@@ -193,6 +197,10 @@
         if k == 0:
             tables()
             put(tgt.at[y], tgt.at[y], R_TGT, across)
+        if k in (1, 2, 3):
+            meet_wait(k - 1)
+            if k < 3:
+                meet_signal(k)
         if k == 2:
             got(craw.at[oy], R_CACHE)
             cache_here.wait()
@@ -428,7 +436,7 @@
             pbuf[k, :, pl.ds(h * 256, 256)] = jnp.dot(left, wog[dest * 2 + h], preferred_element_type=F32).astype(BF)
         return dest
 
-    for k in range(1, 8):
+    for k in (4, 5, 3, 2, 6, 7, 1):
         dest = partial_of(k)
         put(pbuf.at[k], rbuf.at[k], R_RS + k, s, dest)
     lax.fori_loop(17, 32, app_go, 0)
@@ -503,6 +511,7 @@
             pltpu.SemaphoreType.DMA((N_SEND,)),
             pltpu.SemaphoreType.DMA((N_RECV,)),
             pltpu.SemaphoreType.DMA((16,)),
+            pltpu.SemaphoreType.REGULAR((3,)),
         ],
         compiler_params=pltpu.CompilerParams(
             collective_id=0, has_side_effects=True, vmem_limit_bytes=60 * 1024 * 1024),

time: 147 us -> 142 us (0.966); the launches traced: 147 us -> 139 us
  Pallas kernels: 142 us -> 135 us
    pallas_call x1, Pallas kernels: 142 us -> 135 us  [body(): pl.pallas_call(kernel, out_shape=(jax.ShapeDtypeStruct((256, width), BF),...]
where the time goes in v4:
time: 142 us; the launch traced here: 139 us
  Pallas kernels  135 us (95%)
  local copies, waits for them, and re-layouts  3.86 us (3%)
    pallas_call x1, Pallas kernels, body(): pl.pallas_call(kernel, out_shape=(jax.ShapeDtypeStruct((256, width), BF),...  135 us
    unnamed x2, local copies, waits for them, and re-layouts  3.86 us

profile of v4, /device:TPU:53, one launch (start us, length us, event | category | flops | bytes accessed | tf_op | source)
XLA Modules:
  0.0 139.2 jit_solution(11649111115536387172)
XLA Ops:
  0.6 134.7 %shard_map.122 = (bf16[256,512]{1,0:T(8,128)(2,1)}, bf16[2,16,8,2,512]{4,3,2,1,0:T(2,128)(2,1)}) custom-call(s32[4]{0:T(128)} %lens_ref.1, bf16[256,4096]{1,0:T(8,128)(2,1)} %bitcast.6, f32[1,4096]{1,0:T(1,128)} %bitcast.9, f32[1,4096]{1,0:T(1,128)} %bitcast.10, bf16[3,128,512]{2,1,0:T(8,128)(2,1)} %w_ref.1, bf16[512,128]{1,0:T(8,128)(2,1)} %wo_ref.1, ...), custom_call_target="tpu_custom_call" | custom-call | tf_op jit(solution)/shard_map/pallas_call | solution.py:486
  135.4 1.7 %copy.15 = bf16[4,64,512]{2,1,0:T(8,128)(2,1)} copy(bf16[4,64,512]{2,1,0:T(8,128)(2,1)} %bitcast.8) | data formatting | bytes 524288
  137.0 2.2 %copy.16 = bf16[256,2,512]{2,1,0:T(2,128)(2,1)} copy(bf16[256,2,512]{2,1,0:T(2,128)(2,1)} %bitcast.7) | data formatting | bytes 1048576
